TPU v7x, 32 devices: a whole 2x2x4 slice. The times are simulated.
32 devices in a mesh: seq: 4 (over z), row: 2 (over x), col: 4 (over y, core).
Axes of the slice: x: 2, y: 2, z: 4, core: 2. Of those that a mesh axis runs over, the one named last changes fastest.
Arguments:
- grads: bfloat16 [1024, 28672], P('row', ('seq', 'col')), may hold values from -6 to 6
- acts: bfloat16 [1024, 8192], P(('seq', 'col'), 'row'), may hold values from -6 to 6
- out_basis: bfloat16 [28672, 28672], P(('seq', 'col'), 'row'), may hold values from -0.03125 to 0.03125
- in_basis: bfloat16 [8192, 8192], P('row', ('seq', 'col')), may hold values from -0.0625 to 0.0625
- lengths: int32 [4], replicated, may hold values from 1 to 256, 768 in all
Outputs:
- eigenvalues: float32 [28672, 8192], P('row', ('seq', 'col'))
Inputs may be any that keep to these rules, and one draw needn't show every extreme that they name: lengths sum to 768; some sequence is full.
All inputs are finite; a program needn't handle non-finite values.
Results may differ from a plain program's by a relative error of at most 0.0036.
Values may be sent and summed in bfloat16 or wider, within the bound.
No kernel may reach another device: no remote copies, remote signals or barrier semaphores. Data moves between devices by JAX's collectives and lax.ppermute only.
A program may use at most 192 MiB of HBM per device.

v0:
```python
import jax
import jax.numpy as jnp
from jax import lax
from jax.sharding import PartitionSpec as P

SEQ_LEN = 256


def body(grads, acts, out_basis, in_basis, lengths):
    seq_count = lax.axis_size("seq")
    partial_value = jnp.dot(
        lax.all_gather(grads, "row", axis=0, tiled=True),
        out_basis,
        preferred_element_type=jnp.float32,
    )
    shared = lax.psum_scatter(
        partial_value, ("seq", "col"), scatter_dimension=0, tiled=True
    ).astype(jnp.bfloat16)
    grad_proj = lax.all_gather(shared, ("seq", "col"), axis=0, tiled=True)
    act_full = lax.all_gather(acts, ("seq", "col"), axis=0, tiled=True)
    row_count = act_full.shape[0] // lax.axis_size("row")
    act_share = lax.psum_scatter(
        jnp.dot(act_full, in_basis, preferred_element_type=jnp.float32),
        "row",
        scatter_dimension=0,
        tiled=True,
    )
    token_index = lax.axis_index("row") * row_count + jnp.arange(row_count, dtype=jnp.int32)
    seq_owner = token_index // SEQ_LEN
    position = token_index % SEQ_LEN
    seq_ids = jnp.arange(lengths.shape[0], dtype=jnp.int32)
    seq_length = jnp.sum(
        jnp.where(seq_owner[:, None] == seq_ids[None, :], lengths[None, :], 0), axis=1
    )
    is_live = (position < seq_length).astype(jnp.float32)
    act_rows = (act_share * is_live[:, None]).astype(jnp.bfloat16)
    act_proj = lax.all_gather(act_rows, "row", axis=0, tiled=True)
    grad_three = grad_proj.reshape(seq_count, SEQ_LEN, grad_proj.shape[1])
    act_three = act_proj.reshape(seq_count, SEQ_LEN, act_proj.shape[1])

    def accumulate(total, pair):
        grad_seq = lax.dot_general(
            pair[0], pair[1], (((0,), (0,)), ((), ())), preferred_element_type=jnp.float32
        )
        return (total + grad_seq * grad_seq, None)

    start_total = jnp.zeros((grad_proj.shape[1], act_proj.shape[1]), jnp.float32)
    total, unused = lax.scan(accumulate, start_total, (grad_three, act_three))
    return total / (seq_count * SEQ_LEN)


def solution(mesh):
    in_specs = (
        P("row", ("seq", "col")),
        P(("seq", "col"), "row"),
        P(("seq", "col"), "row"),
        P("row", ("seq", "col")),
        P(),
    )
    out_specs = P("row", ("seq", "col"))
    return jax.shard_map(body, mesh=mesh, in_specs=in_specs, out_specs=out_specs, check_vma=False)
```

profile of v0, /device:TPU:0, one launch (start us, length us, event | category | flops | bytes accessed | tf_op | source)
XLA Modules:
  0.0 1026.4 jit_solution(2737312579928235506)
XLA Ops:
  6.5 0.0 all-gather.9.cloned.1.call-start
  6.5 0.7 all-gather.9.cloned.1.call-update
  7.3 0.0 all-gather.5.cloned.1.call-start
  7.3 0.7 all-gather.5.cloned.1.call-update
  8.0 0.0 reduce-scatter.5.cloned.1.call-start
  8.1 78.5 %all-gather.9.cloned.1.call-done = bf16[1024,4096]{1,0:T(8,128)(2,1)} async-done(((bf16[64,4096]{1,0:T(8,128)(2,1)}), bf16[1024,4096]{1,0:T(8,128)(2,1)}) %all-gather.9.cloned.1.call-update) | async-done | bytes 8388624 | tf_op jit(solution)/shard_map/all_gather | solution.py:20
  86.5 10.4 %fusion.11 = f32[1024,512]{1,0:T(8,128)} fusion(bf16[1024,4096]{1,0:T(8,128)(2,1)} %all-gather.9.cloned.1.call-done, bf16[4096,512]{1,0:T(8,128)(2,1)} %param.10), kind=kOutput, calls=%fused_computation.23 | convolution fusion | flops 4294967296 | bytes 14680064 | tf_op jit(solution)/shard_map/dot_general | solution.py:23
  96.9 0.0 reduce-scatter.5.cloned.1.call-update
  97.0 0.0 reduce-scatter.3.cloned.1.call-start
  97.0 40.5 %all-gather.5.cloned.1.call-done = bf16[1024,1792]{1,0:T(8,128)(2,1)} async-done(((bf16[512,1792]{1,0:T(8,128)(2,1)}), bf16[1024,1792]{1,0:T(8,128)(2,1)}) %all-gather.5.cloned.1.call-update) | async-done | bytes 3670032 | tf_op jit(solution)/shard_map/all_gather | solution.py:12
  137.5 61.7 %fusion.10 = f32[1024,14336]{1,0:T(8,128)} fusion(bf16[1024,1792]{1,0:T(8,128)(2,1)} %all-gather.5.cloned.1.call-done, bf16[1792,14336]{1,0:T(8,128)(2,1)} %param.9), kind=kOutput, calls=%fused_computation.22 | convolution fusion | flops 52613349376 | bytes 113770496 | tf_op jit(solution)/shard_map/dot_general | solution.py:11
  199.2 0.0 copy-start
  199.2 0.0 reduce-scatter.3.cloned.1.call-update
  199.3 0.0 all-gather.11.cloned.1.call-start
  199.3 0.6 copy-done
  199.9 0.1 select_reduce_fusion
  200.0 0.0 reduce-scatter.5.cloned.1.call-done
  200.0 2.2 multiply_convert_fusion
  202.2 0.0 all-gather.11.cloned.1.call-update
  202.2 0.0 all-gather.7.cloned.1.call-start
  202.2 538.7 %reduce-scatter.3.cloned.1.call-done = f32[64,14336]{1,0:T(8,128)} async-done(((f32[1024,14336]{1,0:T(8,128)}), f32[64,14336]{1,0:T(8,128)}) %reduce-scatter.3.cloned.1.call-update) | async-done | bytes 3670032 | tf_op jit(solution)/shard_map/reduce_scatter | solution.py:16
  740.9 3.5 convert_element_type.13
  744.4 0.0 all-gather.7.cloned.1.call-update
  744.5 18.3 %all-gather.11.cloned.1.call-done = bf16[1024,512]{1,0:T(8,128)(2,1)} async-done(((bf16[512,512]{1,0:T(8,128)(2,1)}), bf16[1024,512]{1,0:T(8,128)(2,1)}) %all-gather.11.cloned.1.call-update) | async-done | bytes 1048592 | tf_op jit(solution)/shard_map/all_gather | solution.py:37
  762.7 149.8 %all-gather.7.cloned.1.call-done = bf16[1024,14336]{1,0:T(8,128)(2,1)} async-done(((bf16[64,14336]{1,0:T(8,128)(2,1)}), bf16[1024,14336]{1,0:T(8,128)(2,1)}) %all-gather.7.cloned.1.call-update) | async-done | bytes 29360144 | tf_op jit(solution)/shard_map/all_gather | solution.py:19
  912.5 85.2 %while.11 = (s32[]{:T(128)}, f32[14336,512]{1,0:T(8,128)}, bf16[4,256,14336]{2,1,0:T(8,128)(2,1)}, bf16[4,256,512]{2,1,0:T(8,128)(2,1)}, s32[]{:T(128)}, /*index=5*/s32[]{:T(128)}) while((s32[]{:T(128)}, f32[14336,512]{1,0:T(8,128)}, bf16[4,256,14336]{2,1,0:T(8,128)(2,1)}, bf16[4,256,512]{2,1,0:T(8,128)(2,1)}, s32[]{:T(128)}, ...), condition=%wide.region_4.5_spmd.clone, body=%wide.region_3.4_spmd.clone.sunk | while | flops 3780116480 | bytes 66323532 | solution.py:48
  912.5 13.2 %select_add_fusion.2 = f32[14336,512]{1,0:T(8,128)} fusion(f32[14336,512]{1,0:T(8,128)} %get-tuple-element.83, pred[]{:T(512)S(6)} %compare.14, bf16[4,256,14336]{2,1,0:T(8,128)(2,1)} %get-tuple-element.90, s32[]{:T(128)} %get-tuple-element.82, bf16[4,256,512]{2,1,0:T(8,128)(2,1)} %get-tuple-element.91), kind=kOutput, calls=%fused_computation.clone.1 | convolution fusion | flops 3780116480 | bytes 66323456 | tf_op jit(solution)/shard_map/while/body/eval_jaxpr/dot_general | solution.py:42
  925.7 24.0 %select_add_fusion.2 = f32[14336,512]{1,0:T(8,128)} fusion(f32[14336,512]{1,0:T(8,128)} %get-tuple-element.83, pred[]{:T(512)S(6)} %compare.14, bf16[4,256,14336]{2,1,0:T(8,128)(2,1)} %get-tuple-element.90, s32[]{:T(128)} %get-tuple-element.82, bf16[4,256,512]{2,1,0:T(8,128)(2,1)} %get-tuple-element.91), kind=kOutput, calls=%fused_computation.clone.1 | convolution fusion | flops 3780116480 | bytes 66323456 | tf_op jit(solution)/shard_map/while/body/eval_jaxpr/dot_general | solution.py:42
  949.7 24.0 %select_add_fusion.2 = f32[14336,512]{1,0:T(8,128)} fusion(f32[14336,512]{1,0:T(8,128)} %get-tuple-element.83, pred[]{:T(512)S(6)} %compare.14, bf16[4,256,14336]{2,1,0:T(8,128)(2,1)} %get-tuple-element.90, s32[]{:T(128)} %get-tuple-element.82, bf16[4,256,512]{2,1,0:T(8,128)(2,1)} %get-tuple-element.91), kind=kOutput, calls=%fused_computation.clone.1 | convolution fusion | flops 3780116480 | bytes 66323456 | tf_op jit(solution)/shard_map/while/body/eval_jaxpr/dot_general | solution.py:42
  973.7 24.0 %select_add_fusion.2 = f32[14336,512]{1,0:T(8,128)} fusion(f32[14336,512]{1,0:T(8,128)} %get-tuple-element.83, pred[]{:T(512)S(6)} %compare.14, bf16[4,256,14336]{2,1,0:T(8,128)(2,1)} %get-tuple-element.90, s32[]{:T(128)} %get-tuple-element.82, bf16[4,256,512]{2,1,0:T(8,128)(2,1)} %get-tuple-element.91), kind=kOutput, calls=%fused_computation.clone.1 | convolution fusion | flops 3780116480 | bytes 66323456 | tf_op jit(solution)/shard_map/while/body/eval_jaxpr/dot_general | solution.py:42
  997.7 21.9 %broadcast_multiply_fusion = f32[14336,512]{1,0:T(8,128)} fusion(f32[14336,512]{1,0:T(8,128)} %get-tuple-element.27), kind=kLoop, calls=%fused_computation.6 | loop fusion | flops 7340032 | bytes 58720256 | tf_op jit(solution)/shard_map/div | solution.py:49
  (3 shorter events, 0.0 us)
Async XLA Ops:
  6.5 80.0 %all-gather.9.cloned.1.call-start = ((), (), s32[]{:S(2)}) async-start(), calls=%async_computation.5 | async-start | bytes 8912896 | tf_op jit(solution)/shard_map/all_gather | solution.py:20
  7.3 130.3 %all-gather.5.cloned.1.call-start = ((), (), s32[]{:S(2)}) async-start(), calls=%async_computation.2 | async-start | bytes 5505024 | tf_op jit(solution)/shard_map/all_gather | solution.py:12
  8.0 192.0 %reduce-scatter.5.cloned.1.call-start = ((), (), s32[]{:S(2)}) async-start(), calls=%async_computation.6 | async-start | bytes 3145728 | tf_op jit(solution)/shard_map/reduce_scatter | solution.py:22
  97.0 644.0 %reduce-scatter.3.cloned.1.call-start = ((), (), s32[]{:S(2)}) async-start(), calls=%async_computation.3 | async-start | bytes 62390272 | tf_op jit(solution)/shard_map/reduce_scatter | solution.py:16
  199.2 0.7 copy-start
  199.3 563.5 %all-gather.11.cloned.1.call-start = ((), (), s32[]{:S(2)}) async-start(), calls=%async_computation.7 | async-start | bytes 1572864 | tf_op jit(solution)/shard_map/all_gather | solution.py:37
  202.2 710.3 %all-gather.7.cloned.1.call-start = ((), (), s32[]{:S(2)}) async-start(), calls=%async_computation.4 | async-start | bytes 31195136 | tf_op jit(solution)/shard_map/all_gather | solution.py:19
Sparse Core Ops, SparseCore 0:
  9.5 77.0 all-gather.8
  88.1 49.3 all-gather.4
  139.8 31.8 reduce-scatter.4
  199.4 541.5 reduce-scatter.2
  742.3 20.3 all-gather.10
  764.2 148.2 all-gather.6
where the time goes:
time: 1030 us
  waiting for transfers between devices  827 us (80%)
  matrix products  157 us (15%)
  other arithmetic  27.6 us (3%)
  between operations  13.5 us (1%)
    reduce_scatter x1, waiting for transfers between devices, body(): lax.psum_scatter(partial_value, ('seq', 'col'), scatter_dimension=0, tile...  539 us
    all_gather x1, waiting for transfers between devices, body(): grad_proj = lax.all_gather(shared, ('seq', 'col'), axis=0, tiled=True)  150 us
    dot_general x4, matrix products, accumulate(): lax.dot_general(pair[0], pair[1], (((0,), (0,)), ((), ())), preferred_ele...  85.2 us
    all_gather x1, waiting for transfers between devices, body(): act_full = lax.all_gather(acts, ('seq', 'col'), axis=0, tiled=True)  78.5 us
    dot_general x1, matrix products, body(): jnp.dot(lax.all_gather(grads, 'row', axis=0, tiled=True), out_basis, pref...  61.7 us
    all_gather x1, waiting for transfers between devices, body(): lax.all_gather(grads, 'row', axis=0, tiled=True)  40.5 us
    div x1, other arithmetic, body(): return total / (seq_count * SEQ_LEN)  21.9 us
  transfers between devices with their start and end apart: 6, of which 5 were waited for; matrix products, arithmetic and copies ran while one was open for 8% of the time, Pallas kernels for 0%

commit v1 on v0

--- a/solution.py
+++ b/solution.py
@@ -16,7 +16,10 @@
     shared = lax.psum_scatter(
         partial_value, ("seq", "col"), scatter_dimension=0, tiled=True
     ).astype(jnp.bfloat16)
-    grad_proj = lax.all_gather(shared, ("seq", "col"), axis=0, tiled=True)
+    grad_proj = jnp.concatenate(
+        lax.all_to_all(jnp.stack([shared] * lax.axis_size(("seq", "col"))), ("seq", "col"), 0, 0),
+        axis=0,
+    )
     act_full = lax.all_gather(acts, ("seq", "col"), axis=0, tiled=True)
     row_count = act_full.shape[0] // lax.axis_size("row")
     act_share = lax.psum_scatter(

time: 1030 us -> 1480 us (1.44)
  the two profiles are of different devices: /device:TPU:0 before, /device:TPU:13 now
where the time goes in v1:
time: 1480 us
  waiting for transfers between devices  1260 us (85%)
  matrix products  157 us (11%)
  other arithmetic  26.4 us (2%)
    reduce_scatter x1, waiting for transfers between devices, body(): lax.psum_scatter(partial_value, ('seq', 'col'), scatter_dimension=0, tile...  540 us
    all_gather x1, waiting for transfers between devices, body(): act_full = lax.all_gather(acts, ('seq', 'col'), axis=0, tiled=True)  349 us
    all_to_all x1, waiting for transfers between devices, body(): lax.all_to_all(jnp.stack([shared] * lax.axis_size(('seq', 'col'))), ('seq...  232 us
    dot_general x4, matrix products, accumulate(): lax.dot_general(pair[0], pair[1], (((0,), (0,)), ((), ())), preferred_ele...  85.2 us
    reduce_scatter x1, waiting for transfers between devices, body(): lax.psum_scatter(jnp.dot(act_full, in_basis, preferred_element_type=jnp.f...  66.3 us
    dot_general x1, matrix products, body(): jnp.dot(lax.all_gather(grads, 'row', axis=0, tiled=True), out_basis, pref...  61.8 us
    all_gather x1, waiting for transfers between devices, body(): lax.all_gather(grads, 'row', axis=0, tiled=True)  53.4 us
  transfers between devices with their start and end apart: 6, of which 6 were waited for; matrix products, arithmetic and copies ran while one was open for 1% of the time, Pallas kernels for 0%

profile of v1, /device:TPU:13, one launch (start us, length us, event | category | flops | bytes accessed | tf_op | source)
XLA Modules:
  0.0 1479.0 jit_solution(18233097945720318350)
XLA Ops:
  6.5 0.0 all-gather.4.cloned.1.call-start
  6.5 0.7 all-gather.4.cloned.1.call-update
  7.3 0.0 reduce-scatter.3.cloned.1.call-start
  7.3 53.4 %all-gather.4.cloned.1.call-done = bf16[1024,1792]{1,0:T(8,128)(2,1)} async-done(((bf16[512,1792]{1,0:T(8,128)(2,1)}), bf16[1024,1792]{1,0:T(8,128)(2,1)}) %all-gather.4.cloned.1.call-update) | async-done | bytes 3670032 | tf_op jit(solution)/shard_map/all_gather | solution.py:12
  60.7 61.8 %fusion.10 = f32[1024,14336]{1,0:T(8,128)} fusion(bf16[1024,1792]{1,0:T(8,128)(2,1)} %all-gather.4.cloned.1.call-done, bf16[1792,14336]{1,0:T(8,128)(2,1)} %param.9), kind=kOutput, calls=%fused_computation.22 | convolution fusion | flops 52613349376 | bytes 113770496 | tf_op jit(solution)/shard_map/dot_general | solution.py:11
  122.5 0.0 reduce-scatter.3.cloned.1.call-update
  122.5 540.0 %reduce-scatter.3.cloned.1.call-done = f32[64,14336]{1,0:T(8,128)} async-done(((f32[1024,14336]{1,0:T(8,128)}), f32[64,14336]{1,0:T(8,128)}) %reduce-scatter.3.cloned.1.call-update) | async-done | bytes 3670032 | tf_op jit(solution)/shard_map/reduce_scatter | solution.py:16
  662.5 2.2 convert_element_type.13
  664.7 10.1 stack.2
  674.8 8.2 all-to-all-start
  683.0 0.0 copy-start
  683.0 0.0 all-gather.6.cloned.1.call-start
  683.1 0.7 all-gather.6.cloned.1.call-update
  683.8 0.0 reduce-scatter.5.cloned.1.call-start
  683.8 349.4 %all-gather.6.cloned.1.call-done = bf16[1024,4096]{1,0:T(8,128)(2,1)} async-done(((bf16[64,4096]{1,0:T(8,128)(2,1)}), bf16[1024,4096]{1,0:T(8,128)(2,1)}) %all-gather.6.cloned.1.call-update) | async-done | bytes 8388624 | tf_op jit(solution)/shard_map/all_gather | solution.py:23
  1033.2 10.4 fusion.11
  1043.5 0.0 reduce-scatter.5.cloned.1.call-update
  1043.6 0.0 all-gather.8.cloned.1.call-start
  1043.6 0.0 copy-done
  1043.6 0.1 select_reduce_fusion
  1043.7 66.3 %reduce-scatter.5.cloned.1.call-done = f32[512,512]{1,0:T(8,128)} async-done(((f32[1024,512]{1,0:T(8,128)}), f32[512,512]{1,0:T(8,128)}) %reduce-scatter.5.cloned.1.call-update) | async-done | bytes 1048592 | tf_op jit(solution)/shard_map/reduce_scatter | solution.py:25
  1110.0 2.2 multiply_convert_fusion
  1112.2 0.0 all-gather.8.cloned.1.call-update
  1112.2 21.4 %all-gather.8.cloned.1.call-done = bf16[1024,512]{1,0:T(8,128)(2,1)} async-done(((bf16[512,512]{1,0:T(8,128)(2,1)}), bf16[1024,512]{1,0:T(8,128)(2,1)}) %all-gather.8.cloned.1.call-update) | async-done | bytes 1048592 | tf_op jit(solution)/shard_map/all_gather | solution.py:40
  1133.7 231.7 %all-to-all-done = bf16[16,64,14336]{2,1,0:T(8,128)(2,1)} async-done(((bf16[16,64,14336]{2,1,0:T(8,128)(2,1)}), bf16[16,64,14336]{2,1,0:T(8,128)(2,1)}, u32[]{:S(2)}, u32[]{:S(2)}) %all-to-all-start) | async-done | bytes 29360160 | tf_op jit(solution)/shard_map/all_to_all | solution.py:20
  1365.4 85.2 %while.11 = (s32[]{:T(128)}, f32[14336,512]{1,0:T(8,128)}, bf16[4,256,14336]{2,1,0:T(8,128)(2,1)}, bf16[4,256,512]{2,1,0:T(8,128)(2,1)}, s32[]{:T(128)}, /*index=5*/s32[]{:T(128)}) while((s32[]{:T(128)}, f32[14336,512]{1,0:T(8,128)}, bf16[4,256,14336]{2,1,0:T(8,128)(2,1)}, bf16[4,256,512]{2,1,0:T(8,128)(2,1)}, s32[]{:T(128)}, ...), condition=%wide.region_4.5_spmd.clone, body=%wide.region_3.4_spmd.clone.sunk | while | flops 3780116480 | bytes 66323532 | solution.py:51
  1365.4 13.2 select_add_fusion.2
  1378.6 24.0 %select_add_fusion.2 = f32[14336,512]{1,0:T(8,128)} fusion(f32[14336,512]{1,0:T(8,128)} %get-tuple-element.83, pred[]{:T(512)S(6)} %compare.14, bf16[4,256,14336]{2,1,0:T(8,128)(2,1)} %get-tuple-element.90, s32[]{:T(128)} %get-tuple-element.82, bf16[4,256,512]{2,1,0:T(8,128)(2,1)} %get-tuple-element.91), kind=kOutput, calls=%fused_computation.clone.1 | convolution fusion | flops 3780116480 | bytes 66323456 | tf_op jit(solution)/shard_map/while/body/eval_jaxpr/dot_general | solution.py:45
  1402.6 24.0 %select_add_fusion.2 = f32[14336,512]{1,0:T(8,128)} fusion(f32[14336,512]{1,0:T(8,128)} %get-tuple-element.83, pred[]{:T(512)S(6)} %compare.14, bf16[4,256,14336]{2,1,0:T(8,128)(2,1)} %get-tuple-element.90, s32[]{:T(128)} %get-tuple-element.82, bf16[4,256,512]{2,1,0:T(8,128)(2,1)} %get-tuple-element.91), kind=kOutput, calls=%fused_computation.clone.1 | convolution fusion | flops 3780116480 | bytes 66323456 | tf_op jit(solution)/shard_map/while/body/eval_jaxpr/dot_general | solution.py:45
  1426.6 24.0 %select_add_fusion.2 = f32[14336,512]{1,0:T(8,128)} fusion(f32[14336,512]{1,0:T(8,128)} %get-tuple-element.83, pred[]{:T(512)S(6)} %compare.14, bf16[4,256,14336]{2,1,0:T(8,128)(2,1)} %get-tuple-element.90, s32[]{:T(128)} %get-tuple-element.82, bf16[4,256,512]{2,1,0:T(8,128)(2,1)} %get-tuple-element.91), kind=kOutput, calls=%fused_computation.clone.1 | convolution fusion | flops 3780116480 | bytes 66323456 | tf_op jit(solution)/shard_map/while/body/eval_jaxpr/dot_general | solution.py:45
  1450.6 21.9 %broadcast_multiply_fusion = f32[14336,512]{1,0:T(8,128)} fusion(f32[14336,512]{1,0:T(8,128)} %get-tuple-element.27), kind=kLoop, calls=%fused_computation.6 | loop fusion | flops 7340032 | bytes 58720256 | tf_op jit(solution)/shard_map/div | solution.py:52
  (3 shorter events, 0.0 us)
Async XLA Ops:
  6.5 54.1 %all-gather.4.cloned.1.call-start = ((), (), s32[]{:S(2)}) async-start(), calls=%async_computation.3 | async-start | bytes 5505024 | tf_op jit(solution)/shard_map/all_gather | solution.py:12
  7.3 655.2 %reduce-scatter.3.cloned.1.call-start = ((), (), s32[]{:S(2)}) async-start(), calls=%async_computation.4 | async-start | bytes 62390272 | tf_op jit(solution)/shard_map/reduce_scatter | solution.py:16
  674.8 690.5 %all-to-all-start = ((bf16[16,64,14336]{2,1,0:T(8,128)(2,1)}), bf16[16,64,14336]{2,1,0:T(8,128)(2,1)}, u32[]{:S(2)}, u32[]{:S(2)}) async-start(bf16[16,64,14336]{2,1,0:T(8,128)(2,1)} %stack.2), calls=%async_computation.1 | async-start | bytes 58720256 | tf_op jit(solution)/shard_map/all_to_all | solution.py:20
  683.0 360.6 %copy-start = (s32[4]{0:T(128)S(1)}, s32[4]{0:T(128)}, u32[]{:S(2)}) copy-start(s32[4]{0:T(128)} %param.11) | copy-start | bytes 52
  683.0 350.2 %all-gather.6.cloned.1.call-start = ((), (), s32[]{:S(2)}) async-start(), calls=%async_computation.5 | async-start | bytes 8912896 | tf_op jit(solution)/shard_map/all_gather | solution.py:23
  683.8 426.3 %reduce-scatter.5.cloned.1.call-start = ((), (), s32[]{:S(2)}) async-start(), calls=%async_computation.6 | async-start | bytes 3145728 | tf_op jit(solution)/shard_map/reduce_scatter | solution.py:25
  1043.6 90.1 %all-gather.8.cloned.1.call-start = ((), (), s32[]{:S(2)}) async-start(), calls=%async_computation.7 | async-start | bytes 1572864 | tf_op jit(solution)/shard_map/all_gather | solution.py:40
Sparse Core Ops, SparseCore 0:
  8.9 51.7 all-gather.3
  122.6 539.8 reduce-scatter.2
  686.0 347.1 all-gather.5
  1043.7 66.3 reduce-scatter.4
  1112.4 21.2 all-gather.7
